TPU v7x, 32 devices: a whole 2x2x4 slice. The times are simulated.
32 devices in a mesh: rows: 8 (over z, y), modes: 4 (over x, core).
Axes of the slice: x: 2, y: 2, z: 4, core: 2. Of those that a mesh axis runs over, the one named last changes fastest.
Arguments:
- basis: float32 [16384, 16384], P('rows', 'modes'), may hold values from -0.046875 to 0.046875
- blocks: float32 [3, 16384, 256], P(None, ('rows', 'modes')), may hold values from -6 to 6
Outputs:
- projected: float32 [3, 16384, 256], P(None, ('rows', 'modes'))
All inputs are finite; a program needn't handle non-finite values.
Results may differ from a plain program's by a relative error of at most 0.0001.
Values sent between devices are 32-bit elements; how exact they have to be, the bound alone decides.
A program may use at most 192 MiB of HBM per device.

v0:
```python
import jax
import jax.numpy as jnp
from jax import lax
from jax.sharding import PartitionSpec as P


def on_device(basis, blocks):
    highest = lax.Precision.HIGHEST
    results = []
    for block_index in range(blocks.shape[0]):
        partial_value = lax.dot_general(
            basis,
            lax.all_gather(blocks[block_index], "modes", axis=0, tiled=True),
            (((0,), (0,)), ((), ())),
            precision=highest,
            preferred_element_type=jnp.float32,
        )
        summed_block = lax.psum(partial_value, "rows")
        results.append(
            blocks[block_index]
            - lax.psum_scatter(
                jnp.dot(basis, summed_block, precision=highest, preferred_element_type=jnp.float32),
                "modes",
                scatter_dimension=0,
                tiled=True,
            )
        )
    return jnp.stack(results)


def solution(mesh):
    in_specs = (P("rows", "modes"), P(None, ("rows", "modes"), None))
    out_specs = P(None, ("rows", "modes"), None)
    return jax.shard_map(
        on_device, mesh=mesh, in_specs=in_specs, out_specs=out_specs, check_vma=False
    )
```

profile of v0, /device:TPU:0, one launch (start us, length us, event | category | flops | bytes accessed | tf_op | source)
XLA Modules:
  0.0 819.9 jit_solution(15113315749688498149)
XLA Ops:
  6.5 1.5 fusion.9
  8.0 1.0 copy.9
  9.0 0.0 all-gather.11.cloned.1.call-update
  9.0 0.0 all-gather.9.cloned.1.call-start
  9.1 1.0 copy.8
  10.1 0.0 all-gather.9.cloned.1.call-update
  10.1 0.0 all-gather.7.cloned.1.call-start
  10.2 1.0 copy.7
  11.2 0.0 all-gather.7.cloned.1.call-update
  11.2 0.0 all-reduce.3.cloned.1.call-start
  11.3 23.2 %all-gather.11.cloned.1.call-done = f32[1,2048,256]{1,2,0:T(8,128)} async-done(((f32[1,512,256]{1,2,0:T(8,128)}), f32[1,2048,256]{1,2,0:T(8,128)}) %all-gather.11.cloned.1.call-update) | async-done | bytes 2097168 | tf_op jit(solution)/shard_map/all_gather | solution.py:13
  34.5 57.6 %fusion = f32[4096,256]{1,0:T(8,128)} fusion(f32[2048,4096]{1,0:T(8,128)} %param.2, f32[1,2048,256]{1,2,0:T(8,128)} %all-gather.11.cloned.1.call-done), kind=kOutput, calls=%fused_computation.3 | convolution fusion | flops 25769803776 | bytes 39845888 | tf_op jit(solution)/shard_map/dot_general | solution.py:11
  92.0 57.9 %fusion.2 = f32[4096,256]{1,0:T(8,128)} fusion(f32[2048,4096]{1,0:T(8,128)} %param.2, f32[1,2048,256]{1,2,0:T(8,128)} %all-gather.9.cloned.1.call-done), kind=kOutput, calls=%fused_computation.5 | convolution fusion | flops 25769803776 | bytes 39845888 | tf_op jit(solution)/shard_map/dot_general | solution.py:11
  149.9 57.7 %fusion.4 = f32[4096,256]{1,0:T(8,128)} fusion(f32[2048,4096]{1,0:T(8,128)} %param.2, f32[1,2048,256]{1,2,0:T(8,128)} %all-gather.7.cloned.1.call-done), kind=kOutput, calls=%fused_computation.7 | convolution fusion | flops 25769803776 | bytes 39845888 | tf_op jit(solution)/shard_map/dot_general | solution.py:11
  207.6 0.0 all-reduce.3.cloned.1.call-update
  207.7 0.0 reduce-scatter.8.cloned.1.call-start
  207.7 394.9 %all-reduce.3.cloned.1.call-done = (f32[4096,256]{1,0:T(8,128)}, f32[4096,256]{1,0:T(8,128)}, f32[4096,256]{1,0:T(8,128)}) async-done(((f32[4096,256]{1,0:T(8,128)}, f32[4096,256]{1,0:T(8,128)}, f32[4096,256]{1,0:T(8,128)}), (f32[4096,256]{1,0:T(8,128)}, f32[4096,256]{1,0:T(8,128)}, f32[4096,256]{1,0:T(8,128)})) %all-reduce.3.cloned.1.call-update) | async-done | bytes 12582928 | tf_op jit(solution)/shard_map/psum | solution.py:18
  602.6 59.0 %convolution_bitcast_fusion = f32[2048,256]{0,1:T(8,128)} fusion(f32[4096,256]{1,0:T(8,128)} %get-tuple-element.5, f32[2048,4096]{1,0:T(8,128)} %param.2), kind=kOutput, calls=%fused_computation | convolution fusion | flops 25769803776 | bytes 39845888 | tf_op jit(solution)/shard_map/dot_general | solution.py:22
  661.6 0.0 reduce-scatter.4.cloned.1.call-start
  661.6 58.7 %convolution_bitcast_fusion.2 = f32[2048,256]{0,1:T(8,128)} fusion(f32[4096,256]{1,0:T(8,128)} %get-tuple-element.7, f32[2048,4096]{1,0:T(8,128)} %param.2), kind=kOutput, calls=%fused_computation.2 | convolution fusion | flops 25769803776 | bytes 39845888 | tf_op jit(solution)/shard_map/dot_general | solution.py:22
  720.4 0.0 reduce-scatter.4.cloned.1.call-update
  720.4 0.0 reduce-scatter.6.cloned.1.call-start
  720.5 58.9 %convolution_bitcast_fusion.1 = f32[2048,256]{0,1:T(8,128)} fusion(f32[4096,256]{1,0:T(8,128)} %get-tuple-element.6, f32[2048,4096]{1,0:T(8,128)} %param.2), kind=kOutput, calls=%fused_computation.1 | convolution fusion | flops 25769803776 | bytes 39845888 | tf_op jit(solution)/shard_map/dot_general | solution.py:22
  779.3 0.0 reduce-scatter.6.cloned.1.call-update
  779.3 0.0 reduce-scatter.8.cloned.1.call-done
  779.4 1.2 fusion.6
  780.6 0.0 reduce-scatter.4.cloned.1.call-done
  780.6 1.1 fusion.8
  781.7 28.1 %reduce-scatter.6.cloned.1.call-done = f32[512,256]{0,1:T(8,128)} async-done(((f32[2048,256]{0,1:T(8,128)}), f32[512,256]{0,1:T(8,128)}) %reduce-scatter.6.cloned.1.call-update) | async-done | bytes 524304 | tf_op jit(solution)/shard_map/reduce_scatter | solution.py:21
  809.8 1.1 fusion.7
  810.9 0.1 pad_maximum_fusion
  811.0 1.6 copy.6
  (10 shorter events, 0.0 us)
Async XLA Ops:
  6.5 27.9 %all-gather.11.cloned.1.call-start = ((), (), s32[]{:S(2)}) async-start(), calls=%async_computation.8 | async-start | bytes 2621440 | tf_op jit(solution)/shard_map/all_gather | solution.py:13
  9.0 83.0 %all-gather.9.cloned.1.call-start = ((), (), s32[]{:S(2)}) async-start(), calls=%async_computation.7 | async-start | bytes 2621440 | tf_op jit(solution)/shard_map/all_gather | solution.py:13
  10.1 139.8 %all-gather.7.cloned.1.call-start = ((), (), s32[]{:S(2)}) async-start(), calls=%async_computation.6 | async-start | bytes 2621440 | tf_op jit(solution)/shard_map/all_gather | solution.py:13
  11.2 591.3 %all-reduce.3.cloned.1.call-start = ((), (), s32[]{:S(2)}) async-start(), calls=%async_computation.9 | async-start | bytes 25165824 | tf_op jit(solution)/shard_map/psum | solution.py:18
  207.7 571.7 %reduce-scatter.8.cloned.1.call-start = ((), (), s32[]{:S(2)}) async-start(), calls=%async_computation.5 | async-start | bytes 2621440 | tf_op jit(solution)/shard_map/reduce_scatter | solution.py:21
  661.6 119.0 %reduce-scatter.4.cloned.1.call-start = ((), (), s32[]{:S(2)}) async-start(), calls=%async_computation.3 | async-start | bytes 2621440 | tf_op jit(solution)/shard_map/reduce_scatter | solution.py:21
  720.4 89.4 %reduce-scatter.6.cloned.1.call-start = ((), (), s32[]{:S(2)}) async-start(), calls=%async_computation.4 | async-start | bytes 2621440 | tf_op jit(solution)/shard_map/reduce_scatter | solution.py:21
  720.4 58.9 %copy-start.1 = (f32[1,512,256]{1,2,0:T(8,128)S(1)}, f32[1,512,256]{1,2,0:T(8,128)}, u32[]{:S(2)}) copy-start(f32[1,512,256]{1,2,0:T(8,128)} %copy.9) | copy-start | bytes 1572868
  720.5 60.1 %copy-start.2 = (f32[1,512,256]{1,2,0:T(8,128)S(1)}, f32[1,512,256]{1,2,0:T(8,128)}, u32[]{:S(2)}) copy-start(f32[1,512,256]{1,2,0:T(8,128)} %copy.7) | copy-start | bytes 1572868
  779.3 30.5 %copy-start = (f32[1,512,256]{1,2,0:T(8,128)S(1)}, f32[1,512,256]{1,2,0:T(8,128)}, u32[]{:S(2)}) copy-start(f32[1,512,256]{1,2,0:T(8,128)} %copy.8) | copy-start | bytes 1572868
Sparse Core Ops, SparseCore 0:
  9.1 25.2 all-gather.10
  36.0 22.5 all-gather.8
  60.2 22.5 all-gather.6
  207.8 394.7 all-reduce.2
  661.7 30.2 reduce-scatter.7
  720.5 30.2 reduce-scatter.3
  779.5 30.2 reduce-scatter.5
where the time goes:
time: 829 us; the launch traced here: 820 us
  waiting for transfers between devices  446 us (54%)
  matrix products  350 us (42%)
  between operations  13.9 us (2%)
    psum x1, waiting for transfers between devices, on_device(): summed_block = lax.psum(partial_value, 'rows')  395 us
    dot_general x3, matrix products, on_device(): jnp.dot(basis, summed_block, precision=highest, preferred_element_type=jn...  177 us
    dot_general x3, matrix products, on_device(): lax.dot_general(basis, lax.all_gather(blocks[block_index], 'modes', axis=...  173 us
    reduce_scatter x3, waiting for transfers between devices, on_device(): lax.psum_scatter(jnp.dot(basis, summed_block, precision=highest, preferre...  28.1 us
    all_gather x3, waiting for transfers between devices, on_device(): lax.all_gather(blocks[block_index], 'modes', axis=0, tiled=True)  23.2 us
  transfers between devices with their start and end apart: 7, of which 3 were waited for; matrix products, arithmetic and copies ran while one was open for 29% of the time, Pallas kernels for 0%

commit v1 on v0

v1 whole, which is shorter than its diff:
```python
import jax
import jax.numpy as jnp
from jax import lax
from jax.sharding import PartitionSpec as P


def bit_of(axis, bit):
    return (lax.axis_index(axis) // (1 << bit)) % 2


def swap(value, axis, size, bit):
    return lax.ppermute(value, axis, [(i, i ^ (1 << bit)) for i in range(size)])


def levels(size):
    assert size & (size - 1) == 0
    return size.bit_length() - 1


def gather(value, axis, size):
    count = levels(size)
    rows, columns = value.shape
    for at, bit in enumerate(reversed(range(count))):
        mine = bit_of(axis, bit)
        other = swap(value, axis, size, bit)
        value = jnp.stack(
            [jnp.where(mine == 0, value, other), jnp.where(mine == 0, other, value)], axis=at
        )
    return value.reshape(size * rows, columns)


def scatter_sum(value, axis, size):
    count = levels(size)
    rows, columns = value.shape
    value = value.reshape((2,) * count + (rows // size, columns))
    for bit in range(count):
        mine = bit_of(axis, bit)
        at = count - 1 - bit
        sent = lax.dynamic_index_in_dim(value, 1 - mine, at, keepdims=False)
        kept = lax.dynamic_index_in_dim(value, mine, at, keepdims=False)
        value = kept + swap(sent, axis, size, bit)
    return value


def on_device(modes, basis, blocks):
    high = lax.Precision.HIGH
    count = blocks.shape[0]
    partials, summed = [], []
    for index in range(count):
        partials.append(
            lax.dot_general(
                basis,
                gather(blocks[index], "modes", modes),
                (((0,), (0,)), ((), ())),
                precision=high,
                preferred_element_type=jnp.float32,
            )
        )
    for index in range(count):
        partial_value = partials[index]
        if index:
            summed[-1], partial_value = lax.optimization_barrier((summed[-1], partial_value))
        summed.append(lax.psum(partial_value, "rows"))
    results = []
    for index in range(count):
        correction = jnp.dot(
            basis, summed[index], precision=high, preferred_element_type=jnp.float32
        )
        results.append(blocks[index] - scatter_sum(correction, "modes", modes))
    return jnp.stack(results)


def solution(mesh):
    in_specs = (P("rows", "modes"), P(None, ("rows", "modes"), None))
    out_specs = P(None, ("rows", "modes"), None)
    modes = mesh.shape["modes"]

    def run(basis, blocks):
        return on_device(modes, basis, blocks)

    return jax.shard_map(run, mesh=mesh, in_specs=in_specs, out_specs=out_specs, check_vma=False)
```

time: 829 us -> 663 us (0.80)
  matrix products: 350 us -> 120 us
  local copies, waits for them, and re-layouts: 6.14 us -> 53.3 us
  other arithmetic: 3.53 us -> 16 us
    dot_general x6, matrix products: 350 us -> 120 us  [the longest x3 60.4 us: on_device(): lax.dot_general(basis, gather(blocks[index], 'modes', modes), (((0,), (0,...]
    ppermute x0 -> x12, waiting for transfers between devices: none -> 70.3 us  [swap(): return lax.ppermute(value, axis, [(i, i ^ 1 << bit) for i in range(size)])]
    reduce_scatter x3 -> x0, waiting for transfers between devices: 28.1 us -> none  [on_device(): lax.psum_scatter(jnp.dot(basis, summed_block, precision=highest, preferre...]
    all_gather x3 -> x0, waiting for transfers between devices: 23.2 us -> none  [on_device(): lax.all_gather(blocks[block_index], 'modes', axis=0, tiled=True)]
    psum x1 -> x3, waiting for transfers between devices: 395 us -> 375 us  [on_device(): summed.append(lax.psum(partial_value, 'rows'))]
    unnamed x9 -> x16, local copies, waits for them, and re-layouts: 3.07 us -> 21 us
    dynamic_slice x0 -> x2, local copies, waits for them, and re-layouts: none -> 14 us  [scatter_sum(): kept = lax.dynamic_index_in_dim(value, mine, at, keepdims=False)]
    reshape x0 -> x3, local copies, waits for them, and re-layouts: none -> 12 us  [scatter_sum(): value = value.reshape((2,) * count + (rows // size, columns))]
  transfers between devices with their start and end apart: 7 -> 15, of which waited for: 3 -> 12; matrix products, arithmetic and copies ran while one was open for 29% -> 14% of each run, Pallas kernels for 0% -> 0%
where the time goes in v1:
time: 663 us; the launch traced here: 657 us
  waiting for transfers between devices  446 us (67%)
  matrix products  120 us (18%)
  local copies, waits for them, and re-layouts  53.3 us (8%)
  other arithmetic  16 us (2%)
  between operations  13.5 us (2%)
  starting transfers between devices  8.49 us (1%)
    psum x3, waiting for transfers between devices, on_device(): summed.append(lax.psum(partial_value, 'rows'))  375 us
    ppermute x12, waiting for transfers between devices, swap(): return lax.ppermute(value, axis, [(i, i ^ 1 << bit) for i in range(size)])  70.3 us
    dot_general x3, matrix products, on_device(): lax.dot_general(basis, gather(blocks[index], 'modes', modes), (((0,), (0,...  60.4 us
    dot_general x3, matrix products, on_device(): jnp.dot(basis, summed[index], precision=high, preferred_element_type=jnp....  59.7 us
    unnamed x16, local copies, waits for them, and re-layouts  21 us
    dynamic_slice x2, local copies, waits for them, and re-layouts, scatter_sum(): kept = lax.dynamic_index_in_dim(value, mine, at, keepdims=False)  14 us
  transfers between devices with their start and end apart: 15, of which 12 were waited for; matrix products, arithmetic and copies ran while one was open for 14% of the time, Pallas kernels for 0%

profile of v1, /device:TPU:0, one launch (start us, length us, event | category | flops | bytes accessed | tf_op | source)
XLA Modules:
  0.0 657.2 jit_solution(16323626238561715177)
XLA Ops:
  6.5 2.4 slice_bitcast_fusion
  8.9 3.0 collective-permute-start
  11.9 12.7 %collective-permute-done = f32[512,256]{1,0:T(8,128)S(1)} collective-permute-done((f32[512,256]{1,0:T(8,128)S(1)}, f32[512,256]{1,0:T(8,128)S(1)}, u32[]{:S(2)}, u32[]{:S(2)}) %collective-permute-start) | collective-permute-done | bytes 524320 | tf_op jit(solution)/shard_map/ppermute | solution.py:12
  25.4 9.7 %collective-permute-done.2 = f32[512,256]{1,0:T(8,128)} collective-permute-done((f32[512,256]{1,0:T(8,128)S(1)}, f32[512,256]{1,0:T(8,128)}, u32[]{:S(2)}, u32[]{:S(2)}) %collective-permute-start.2) | collective-permute-done | bytes 524320 | tf_op jit(solution)/shard_map/ppermute | solution.py:12
  38.4 3.0 collective-permute-done.1
  44.4 19.9 %convolution_bitcast_fusion.2 = f32[4096,256]{0,1:T(8,128)} fusion(f32[2048,256]{1,0:T(8,128)} %bitcast.122, f32[2048,4096]{1,0:T(8,128)} %param.2), kind=kOutput, calls=%fused_computation.2 | convolution fusion | flops 12884901888 | bytes 39845888 | tf_op jit(solution)/shard_map/dot_general | solution.py:51
  65.6 2.9 collective-permute-done.3
  71.4 20.4 %convolution_bitcast_fusion.1 = f32[4096,256]{0,1:T(8,128)} fusion(f32[2048,256]{1,0:T(8,128)} %bitcast.123, f32[2048,4096]{1,0:T(8,128)} %param.2), kind=kOutput, calls=%fused_computation.1 | convolution fusion | flops 12884901888 | bytes 39845888 | tf_op jit(solution)/shard_map/dot_general | solution.py:51
  91.8 130.5 %all-reduce.4.cloned.1.call-done = f32[4096,256]{0,1:T(8,128)} async-done(((f32[4096,256]{0,1:T(8,128)}), f32[4096,256]{0,1:T(8,128)}) %all-reduce.4.cloned.1.call-update) | async-done | bytes 4194320 | tf_op jit(solution)/shard_map/psum | solution.py:63
  222.4 19.6 %convolution_bitcast_fusion.5 = f32[2048,256]{0,1:T(8,128)} fusion(f32[4096,256]{0,1:T(8,128)} %all-reduce.4.cloned.1.call-done, f32[2048,4096]{1,0:T(8,128)} %param.2), kind=kOutput, calls=%fused_computation.5 | convolution fusion | flops 12884901888 | bytes 39845888 | tf_op jit(solution)/shard_map/dot_general | solution.py:66
  241.9 4.0 reshape.20
  245.9 5.3 constant_dynamic-slice_fusion.5
  251.3 3.6 copy.13
  256.4 2.1 copy.12
  262.2 7.7 %collective-permute-done.6 = f32[512,256]{1,0:T(8,128)S(1)} collective-permute-done((f32[512,256]{1,0:T(8,128)}, f32[512,256]{1,0:T(8,128)S(1)}, u32[]{:S(2)}, u32[]{:S(2)}) %collective-permute-start.6) | collective-permute-done | bytes 524320 | tf_op jit(solution)/shard_map/ppermute | solution.py:12
  270.7 10.1 %collective-permute-done.5 = f32[512,256]{1,0:T(8,128)} collective-permute-done((f32[512,256]{1,0:T(8,128)}, f32[512,256]{1,0:T(8,128)}, u32[]{:S(2)}, u32[]{:S(2)}) %collective-permute-start.5) | collective-permute-done | bytes 524320 | tf_op jit(solution)/shard_map/ppermute | solution.py:12
  282.3 2.6 collective-permute-done.7
  286.8 20.1 %convolution_bitcast_fusion = f32[4096,256]{0,1:T(8,128)} fusion(f32[2048,256]{1,0:T(8,128)} %bitcast.124, f32[2048,4096]{1,0:T(8,128)} %param.2), kind=kOutput, calls=%fused_computation | convolution fusion | flops 12884901888 | bytes 39845888 | tf_op jit(solution)/shard_map/dot_general | solution.py:51
  306.9 110.3 %all-reduce.6.cloned.1.call-done = f32[4096,256]{0,1:T(8,128)} async-done(((f32[4096,256]{0,1:T(8,128)}), f32[4096,256]{0,1:T(8,128)}) %all-reduce.6.cloned.1.call-update) | async-done | bytes 4194320 | tf_op jit(solution)/shard_map/psum | solution.py:63
  417.2 20.3 %convolution_bitcast_fusion.4 = f32[2048,256]{0,1:T(8,128)} fusion(f32[4096,256]{0,1:T(8,128)} %all-reduce.6.cloned.1.call-done, f32[2048,4096]{1,0:T(8,128)} %param.2), kind=kOutput, calls=%fused_computation.4 | convolution fusion | flops 12884901888 | bytes 39845888 | tf_op jit(solution)/shard_map/dot_general | solution.py:66
  437.5 4.0 reshape.22
  441.5 134.7 %all-reduce.8.cloned.1.call-done = f32[4096,256]{0,1:T(8,128)} async-done(((f32[4096,256]{0,1:T(8,128)}), f32[4096,256]{0,1:T(8,128)}) %all-reduce.8.cloned.1.call-update) | async-done | bytes 4194320 | tf_op jit(solution)/shard_map/psum | solution.py:63
  576.2 19.8 %convolution_bitcast_fusion.3 = f32[2048,256]{0,1:T(8,128)} fusion(f32[4096,256]{0,1:T(8,128)} %all-reduce.8.cloned.1.call-done, f32[2048,4096]{1,0:T(8,128)} %param.2), kind=kOutput, calls=%fused_computation.3 | convolution fusion | flops 12884901888 | bytes 39845888 | tf_op jit(solution)/shard_map/dot_general | solution.py:66
  596.0 4.0 reshape.23
  600.0 8.6 %constant_dynamic-slice_fusion.1 = (f32[2,1,512,256]{2,1,0,3:T(1,128)}, f32[2,1,512,256]{2,1,0,3:T(1,128)}, f32[2,1,512,256]{2,1,0,3:T(1,128)}, f32[2,1,512,256]{2,1,0,3:T(1,128)S(1)}) fusion(f32[2,2,512,256]{2,1,0,3:T(2,128)} %reshape.23, s32[]{:T(128)S(6)} %select_n.137, s32[]{:T(128)S(6)} %select_n.138, f32[2,2,512,256]{2,1,0,3:T(2,128)} %reshape.22), kind=kLoop, calls=%fused_computation.44 | loop fusion | bytes 8388616 | tf_op jit(solution)/shard_map/jit(dynamic_index_in_dim)/dynamic_slice | solution.py:40
  608.6 3.6 copy.17
  612.2 3.6 copy.15
  616.3 3.6 copy.16
  620.0 2.1 copy.14
  622.1 1.8 bitcast_add_fusion
  627.5 11.3 %collective-permute-done.11 = f32[512,256]{1,0:T(8,128)S(1)} collective-permute-done((f32[512,256]{1,0:T(8,128)S(1)}, f32[512,256]{1,0:T(8,128)S(1)}, u32[]{:S(2)}, u32[]{:S(2)}) %collective-permute-start.11) | collective-permute-done | bytes 524320 | tf_op jit(solution)/shard_map/ppermute | solution.py:12
  638.7 10.3 %collective-permute-done.9 = f32[512,256]{1,0:T(8,128)S(1)} collective-permute-done((f32[512,256]{1,0:T(8,128)S(1)}, f32[512,256]{1,0:T(8,128)S(1)}, u32[]{:S(2)}, u32[]{:S(2)}) %collective-permute-start.9) | collective-permute-done | bytes 524320 | tf_op jit(solution)/shard_map/ppermute | solution.py:12
  (50 shorter events, 26.1 us)
Async XLA Ops:
  6.5 28.6 %copy-start = (f32[3,512,256]{2,1,0:T(8,128)S(1)}, f32[3,512,256]{2,1,0:T(8,128)}, u32[]{:S(2)}) copy-start(f32[3,512,256]{2,1,0:T(8,128)} %param.3) | copy-start | bytes 4718596
  6.5 215.8 %all-reduce.4.cloned.1.call-start = ((), (), s32[]{:S(2)}) async-start(), calls=%async_computation | async-start | bytes 8388608 | tf_op jit(solution)/shard_map/psum | solution.py:63
  8.9 15.7 %collective-permute-start = (f32[512,256]{1,0:T(8,128)S(1)}, f32[512,256]{1,0:T(8,128)S(1)}, u32[]{:S(2)}, u32[]{:S(2)}) collective-permute-start(f32[512,256]{1,0:T(8,128)S(1)} %get-tuple-element.35), channel_id=1, source_target_pairs={{0,2},{1,3},{2,0},{3,1},{4,6},{5,7},{6,4},{7,5},{8,10},{9,11},{10,... | collective-permute-start | bytes 1572872 | tf_op jit(solution)/shard_map/ppermute | solution.py:12
  11.9 23.3 %collective-permute-start.2 = (f32[512,256]{1,0:T(8,128)S(1)}, f32[512,256]{1,0:T(8,128)}, u32[]{:S(2)}, u32[]{:S(2)}) collective-permute-start(f32[512,256]{1,0:T(8,128)S(1)} %get-tuple-element.36), channel_id=1, source_target_pairs={{0,2},{1,3},{2,0},{3,1},{4,6},{5,7},{6,4},{7,5},{8,10},{9,11},{10,... | collective-permute-start | bytes 1572872 | tf_op jit(solution)/shard_map/ppermute | solution.py:12
  24.7 0.8 copy-start.3
  36.5 0.8 copy-start.1
  38.4 3.0 collective-permute-start.1
  64.3 352.8 %all-reduce.6.cloned.1.call-start = ((), (), s32[]{:S(2)}) async-start(), calls=%async_computation.1 | async-start | bytes 8388608 | tf_op jit(solution)/shard_map/psum | solution.py:63
  65.4 3.0 collective-permute-start.3
  254.9 3.6 collective-permute-start.4
  254.9 15.0 %collective-permute-start.6 = (f32[512,256]{1,0:T(8,128)}, f32[512,256]{1,0:T(8,128)S(1)}, u32[]{:S(2)}, u32[]{:S(2)}) collective-permute-start(f32[512,256]{1,0:T(8,128)} %get-tuple-element.34), channel_id=1, source_target_pairs={{0,2},{1,3},{2,0},{3,1},{4,6},{5,7},{6,4},{7,5},{8,10},{9,11},{10,... | collective-permute-start | bytes 1572872 | tf_op jit(solution)/shard_map/ppermute | solution.py:12
  261.1 19.7 %collective-permute-start.5 = (f32[512,256]{1,0:T(8,128)}, f32[512,256]{1,0:T(8,128)}, u32[]{:S(2)}, u32[]{:S(2)}) collective-permute-start(f32[512,256]{1,0:T(8,128)} %dynamic-slice_bitcast_fusion.2), channel_id=1, source_target_pairs={{0,2},{1,3},{2,0},{3,1},{4,6},{5,7},{6,4},{7,5},{8,10},{9,11},{10,... | collective-permute-start | bytes 1572872 | tf_op jit(solution)/shard_map/ppermute | solution.py:12
  262.0 314.3 %all-reduce.8.cloned.1.call-start = ((), (), s32[]{:S(2)}) async-start(), calls=%async_computation.2 | async-start | bytes 8388608 | tf_op jit(solution)/shard_map/psum | solution.py:63
  269.9 0.8 copy-start.4
  282.3 2.7 collective-permute-start.7
  612.2 9.8 %collective-permute-start.10 = (f32[2,512,256]{2,1,0:T(8,128)}, f32[2,512,256]{2,1,0:T(8,128)}, u32[]{:S(2)}, u32[]{:S(2)}) collective-permute-start(f32[2,512,256]{2,1,0:T(8,128)} %bitcast.127), channel_id=1, source_target_pairs={{0,1},{1,0},{2,3},{3,2},{4,5},{5,4},{6,7},{7,6},{8,9},{9,8},{10,11... | collective-permute-start | bytes 3145736 | tf_op jit(solution)/shard_map/ppermute | solution.py:12
  615.8 9.6 %collective-permute-start.8 = (f32[2,512,256]{2,1,0:T(8,128)}, f32[2,512,256]{2,1,0:T(8,128)}, u32[]{:S(2)}, u32[]{:S(2)}) collective-permute-start(f32[2,512,256]{2,1,0:T(8,128)} %bitcast.126), channel_id=1, source_target_pairs={{0,1},{1,0},{2,3},{3,2},{4,5},{5,4},{6,7},{7,6},{8,9},{9,8},{10,11... | collective-permute-start | bytes 3145736 | tf_op jit(solution)/shard_map/ppermute | solution.py:12
  622.1 3.4 copy-start.2
  623.9 14.9 %collective-permute-start.11 = (f32[512,256]{1,0:T(8,128)S(1)}, f32[512,256]{1,0:T(8,128)S(1)}, u32[]{:S(2)}, u32[]{:S(2)}) collective-permute-start(f32[512,256]{1,0:T(8,128)S(1)} %dynamic-slice_bitcast_fusion), channel_id=1, source_target_pairs={{0,2},{1,3},{2,0},{3,1},{4,6},{5,7},{6,4},{7,5},{8,10},{9,11},{10,... | collective-permute-start | bytes 1572872 | tf_op jit(solution)/shard_map/ppermute | solution.py:12
  626.8 22.2 %collective-permute-start.9 = (f32[512,256]{1,0:T(8,128)S(1)}, f32[512,256]{1,0:T(8,128)S(1)}, u32[]{:S(2)}, u32[]{:S(2)}) collective-permute-start(f32[512,256]{1,0:T(8,128)S(1)} %dynamic-slice_bitcast_fusion.1), channel_id=1, source_target_pairs={{0,2},{1,3},{2,0},{3,1},{4,6},{5,7},{6,4},{7,5},{8,10},{9,11},{10,... | collective-permute-start | bytes 1572872 | tf_op jit(solution)/shard_map/ppermute | solution.py:12
Sparse Core Ops, SparseCore 0:
  64.5 157.8 all-reduce.3
  262.1 155.0 all-reduce.5
  420.8 155.3 all-reduce.7
